TPU v7x, 256 devices: a whole 4x4x8 slice. The times are simulated.
256 devices in a mesh: wide: 64 (over y, z, core), narrow: 4 (over x).
Axes of the slice: x: 4, y: 4, z: 8, core: 2. Of those that a mesh axis runs over, the one named last changes fastest.
Arguments:
- diag_block: float32 [256, 512, 512], P('wide', None, 'narrow'), as said below
- panel: float32 [256, 1024, 512], P('wide', None, 'narrow'), may hold values from -2 to 2
- panel_count: int32 [256], P('wide'), may hold values from 1 to 8, 1152 in all
- pair_owner: int32 [9216, 1], P('wide'), may hold values from 0 to 63; in each aligned block of 144 rows (0 to 143, 144 to 287, ...) at most 3 rows name the same one
- pair_slot: int32 [9216], P('wide'), may hold values from 0 to 7
- ancestor: float32 [512, 128, 128], P(('wide', 'narrow')), may hold values from -6 to 6
Outputs:
- factor: float32 [256, 512, 512], P('wide', None, 'narrow')
- lower_panel: float32 [256, 1024, 512], P('wide', None, 'narrow')
- updated: float32 [512, 128, 128], P(('wide', 'narrow'))
Inputs may be any that keep to these rules, and one draw needn't show every extreme that they name: Each diag_block[s] is symmetric, and its least eigenvalue is 0.2 or more. `pair_owner`: among the rows of one index of wide no owner is named more than 3 times, a bound that some block reaches.
All inputs are finite; a program needn't handle non-finite values. No bound on the sum of `panel_count` on one device may be relied on, other than what follows from the above.
Results may differ from a plain program's by a relative error of at most 0.00016.
Values sent between devices are 32-bit elements; how exact they have to be, the bound alone decides.
A program may use at most 128 MiB of HBM per device.

v0:
```python
import jax
import jax.numpy as jnp
import numpy as np
from jax import lax
from jax.sharding import PartitionSpec as P

W = 512
B = 128
P_SIZE = 8
T_DEV = 2


def pair_lists(count):
    first = []
    second = []
    for outer in range(count):
        for inner in range(outer + 1):
            first.append(outer)
            second.append(inner)
    return (np.array(first, np.int32), np.array(second, np.int32))


def local(diag_block, panel, panel_count, pair_owner, pair_slot, ancestor):
    supers_here = diag_block.shape[0]
    col_width = diag_block.shape[2]
    narrow_index = lax.axis_index("narrow")
    narrow_count = lax.axis_size("narrow")
    wide_count = lax.axis_size("wide")
    col_start = narrow_index * col_width
    whole_diag = lax.all_gather(diag_block, "narrow", axis=2, tiled=True)
    factor = jnp.linalg.cholesky(whole_diag)
    identity = jnp.broadcast_to(jnp.eye(W, dtype=jnp.float32), factor.shape)
    inverse = lax.linalg.triangular_solve(factor, identity, left_side=True, lower=True)
    inverse_t = jnp.swapaxes(inverse, 1, 2)
    own_cols = lax.dynamic_slice_in_dim(inverse_t, col_start, col_width, 2)
    lower_panel = jnp.einsum(
        "srk,skc->src",
        lax.all_gather(panel, "narrow", axis=2, tiled=True),
        own_cols,
        precision=lax.Precision.HIGHEST,
    )
    block_index = jnp.arange(P_SIZE * B, dtype=jnp.int32) // B
    live = (block_index[None, :] < panel_count[:, None]).astype(jnp.float32)
    lower_panel = lower_panel * live[:, :, None]
    first, second = pair_lists(P_SIZE)
    blocks = lower_panel.reshape(supers_here, P_SIZE, B, col_width)
    partial_updates = jnp.einsum(
        "spac,spbc->spab", blocks[:, first], blocks[:, second], precision=lax.Precision.HIGHEST
    )
    pair_rows = supers_here * len(first)
    partial_updates = partial_updates.reshape(pair_rows, B, B)
    capacity = max(2, (pair_rows + wide_count - 1) // wide_count)
    owners = pair_owner[:, 0]
    owner_table = (owners[:, None] == jnp.arange(wide_count, dtype=jnp.int32)[None, :]).astype(
        jnp.int32
    )
    earlier = jnp.cumsum(owner_table, axis=0) - owner_table
    rank_here = jnp.sum(earlier * owner_table, axis=1)
    position = owners * capacity + rank_here
    buffer_rows = wide_count * capacity
    row_slots = T_DEV * narrow_count
    slot_ids = jnp.full((buffer_rows,), -1, jnp.int32).at[position].set(pair_slot)
    send_buffer = jnp.zeros((buffer_rows, B, B), jnp.float32).at[position].set(partial_updates)
    received, got_slots = (
        lax.all_to_all(send_buffer, "wide", split_axis=0, concat_axis=0, tiled=True),
        lax.all_to_all(slot_ids, "wide", split_axis=0, concat_axis=0, tiled=True),
    )
    slot_table = (got_slots[:, None] == jnp.arange(row_slots, dtype=jnp.int32)[None, :]).astype(
        jnp.float32
    )
    row_sums = jnp.einsum("ri,rab->iab", slot_table, received, precision=lax.Precision.HIGHEST)
    summed = lax.psum_scatter(row_sums, "narrow", scatter_dimension=0, tiled=True)
    factor_cols = lax.dynamic_slice_in_dim(factor, col_start, col_width, 2)
    return (factor_cols, lower_panel, ancestor - summed)


def solution(mesh):
    placed = (
        P("wide", None, "narrow"),
        P("wide", None, "narrow"),
        P("wide"),
        P("wide", None),
        P("wide"),
        P(("wide", "narrow"), None, None),
    )
    return jax.shard_map(
        local,
        mesh=mesh,
        in_specs=placed,
        out_specs=(
            P("wide", None, "narrow"),
            P("wide", None, "narrow"),
            P(("wide", "narrow"), None, None),
        ),
        check_vma=False,
    )
```

profile of v0, /device:TPU:8, one launch (start us, length us, event | category | flops | bytes accessed | tf_op | source)
XLA Modules:
  0.0 1013.3 jit_solution(1670821156970173186)
XLA Ops:
  13.6 12.4 %all-to-all-start = ((s32[64,3,1]{1,2,0:T(1,128)}), s32[64,3,1]{1,2,0:T(1,128)S(1)}, u32[]{:S(2)}, u32[]{:S(2)}) async-start(s32[64,3,1]{1,2,0:T(1,128)} %bitcast.20), calls=%async_computation | async-start | bytes 65536 | tf_op jit(solution)/shard_map/all_to_all | solution.py:66
  27.2 36.9 %all-gather.3.cloned.1.call-done = f32[4,512,512]{1,2,0:T(8,128)} async-done(((f32[4,512,128]{1,2,0:T(8,128)}), f32[4,512,512]{1,2,0:T(8,128)}) %all-gather.3.cloned.1.call-update) | async-done | bytes 4194320 | tf_op jit(solution)/shard_map/all_gather | solution.py:30
  64.1 5.3 copy.75
  69.4 4.5 fusion.5
  75.9 46.9 %custom-call.34 = f32[4,128,128]{2,1,0:T(8,128)S(1)} custom-call(f32[4,128,128]{2,1,0:T(8,128)S(1)} %cholesky.274), custom_call_target="Cholesky" | custom-call | tf_op jit(solution)/shard_map/jit(cholesky)/cholesky | solution.py:31
  122.8 39.3 %custom-call.35 = f32[4,1,128,128]{2,3,1,0:T(8,128)S(1)} custom-call(f32[4,1,128,128]{3,2,1,0:T(8,128)S(1)} %select_bitcast_fusion.2), custom_call_target="InvertDiagBlocksLowerTriangular" | custom-call | tf_op jit(solution)/shard_map/jit(cholesky)/cholesky | solution.py:31
  169.6 47.1 %custom-call.36 = f32[4,128,128]{2,1,0:T(8,128)S(1)} custom-call(f32[4,128,128]{2,1,0:T(8,128)S(1)} %cholesky.278), custom_call_target="Cholesky" | custom-call | tf_op jit(solution)/shard_map/jit(cholesky)/cholesky | solution.py:31
  217.6 39.3 %custom-call.37 = f32[4,1,128,128]{2,3,1,0:T(8,128)S(1)} custom-call(f32[4,1,128,128]{3,2,1,0:T(8,128)S(1)} %get-tuple-element.46), custom_call_target="InvertDiagBlocksLowerTriangular" | custom-call | tf_op jit(solution)/shard_map/jit(cholesky)/cholesky | solution.py:31
  260.9 46.9 %custom-call.38 = f32[4,128,128]{2,1,0:T(8,128)S(1)} custom-call(f32[4,128,128]{2,1,0:T(8,128)S(1)} %cholesky.283), custom_call_target="Cholesky" | custom-call | tf_op jit(solution)/shard_map/jit(cholesky)/cholesky | solution.py:31
  308.6 39.8 %custom-call.39 = f32[4,1,128,128]{2,3,1,0:T(8,128)S(1)} custom-call(f32[4,1,128,128]{3,2,1,0:T(8,128)S(1)} %get-tuple-element.44), custom_call_target="InvertDiagBlocksLowerTriangular" | custom-call | tf_op jit(solution)/shard_map/jit(cholesky)/cholesky | solution.py:31
  352.1 46.9 %custom-call.40 = f32[4,128,128]{2,1,0:T(8,128)S(1)} custom-call(f32[4,128,128]{2,1,0:T(8,128)S(1)} %convolution_subtract_fusion.3), custom_call_target="Cholesky" | custom-call | tf_op jit(solution)/shard_map/jit(cholesky)/cholesky | solution.py:31
  400.2 6.7 broadcast_select_fusion
  406.9 15.0 %while.1 = (s32[]{:T(128)}, f32[4,512,512]{2,1,0:T(8,128)}, s32[4,2]{0,1:T(2,128)S(1)}, f32[4,4,128,128]{3,2,0,1:T(8,128)}, s32[]{:T(128)}) while((s32[]{:T(128)}, f32[4,512,512]{2,1,0:T(8,128)}, s32[4,2]{0,1:T(2,128)S(1)}, f32[4,4,128,128]{3,2,0,1:T(8,128)}, s32[]{:T(128)}) %tuple.40), condition=%wide.while_cond, body=%wide.while_body.sunk | while | flops 2 | bytes 525421 | solution.py:33
  421.9 158.2 %custom-call.41 = f32[4,4,128,128]{2,3,1,0:T(8,128)S(1)} custom-call(f32[4,4,128,128]{3,2,1,0:T(8,128)} %bitcast.100), custom_call_target="InvertDiagBlocksLowerTriangular" | custom-call | tf_op jit(solution)/shard_map/triangular_solve | solution.py:33
  595.1 13.3 %multiply_bitcast_fusion = f32[4,1024,128]{1,2,0:T(8,128)} fusion(f32[4,1024,512]{2,1,0:T(8,128)} %all-gather.5.cloned.1.call-done, s32[]{:T(128)S(6)} %select_n.29, f32[4,128,512]{2,1,0:T(8,128)S(1)} %fusion.35, f32[4,128,512]{2,1,0:T(8,128)S(1)} %fusion.40, f32[4,128,512]{2,1,0:T(8,128)S(1)} %fusion.38, f32[4,128,512]{2,1,0:T(8,128)} %fusion.37, ...), kind=kOutput, calls=%fused_computation.28 | convolution fusion | flops 3222536192 | bytes 14696452 | tf_op jit(solution)/shard_map/srk,skc->src/dot_general | solution.py:36
  610.3 6.7 gather_fusion.1
  617.1 6.7 gather_fusion
  623.8 25.8 %fusion.2 = f32[4,36,128,128]{3,2,1,0:T(8,128)} fusion(f32[36,4,128,128]{3,2,1,0:T(8,128)} %gather_fusion.1, f32[36,4,128,128]{3,2,1,0:T(8,128)} %gather_fusion), kind=kOutput, calls=%fused_computation.8 | convolution fusion | flops 3623878656 | bytes 28311552 | tf_op jit(solution)/shard_map/spac,spbc->spab/dot_general | solution.py:47
  649.6 6.2 broadcast_in_dim.43
  655.7 26.3 %scatter_fusion = f32[192,128,128]{2,1,0:T(8,128)} fusion(f32[192,128,128]{2,1,0:T(8,128)} %broadcast_in_dim.43, s32[144]{0:T(256)S(1)} %bitcast.98, f32[144,128,128]{2,1,0:T(8,128)} %bitcast.94), kind=kCustom, calls=%fused_computation.3 | custom fusion | bytes 28312128 | tf_op jit(solution)/shard_map/scatter | solution.py:63
  682.1 10.7 %all-to-all-start.1 = ((f32[192,128,128]{2,1,0:T(8,128)}), f32[192,128,128]{2,1,0:T(8,128)}, u32[]{:S(2)}, u32[]{:S(2)}) async-start(f32[192,128,128]{2,1,0:T(8,128)} %scatter_fusion), calls=%async_computation.1 | async-start | bytes 25165824 | tf_op jit(solution)/shard_map/all_to_all | solution.py:65
  694.2 273.1 %all-to-all-done.1 = f32[192,128,128]{2,1,0:T(8,128)} async-done(((f32[192,128,128]{2,1,0:T(8,128)}), f32[192,128,128]{2,1,0:T(8,128)}, u32[]{:S(2)}, u32[]{:S(2)}) %all-to-all-start.1) | async-done | bytes 12582944 | tf_op jit(solution)/shard_map/all_to_all | solution.py:65
  967.4 15.5 %fusion = f32[8,128,128]{2,0,1:T(8,128)S(1)} fusion(f32[192,128,128]{2,1,0:T(8,128)} %all-to-all-done.1, s32[192]{0:T(256)S(1)} %eq.54), kind=kOutput, calls=%fused_computation.6 | convolution fusion | flops 301991424 | bytes 13107968 | tf_op jit(solution)/shard_map/ri,rab->iab/dot_general | solution.py:71
  986.0 18.7 %reduce-scatter.2.cloned.1.call-done = f32[2,128,128]{2,1,0:T(8,128)} async-done(((f32[8,128,128]{2,1,0:T(8,128)}), f32[2,128,128]{2,1,0:T(8,128)}) %reduce-scatter.2.cloned.1.call-update) | async-done | bytes 131088 | tf_op jit(solution)/shard_map/reduce_scatter | solution.py:72
  (91 shorter events, 65.4 us)
Async XLA Ops:
  7.2 18.9 %copy-start.6 = (s32[36]{0:T(128)S(1)}, s32[36]{0:T(128)}, u32[]{:S(2)}) copy-start(s32[36]{0:T(128)} %constant.237) | copy-start | bytes 436
  7.2 18.9 %copy-start.5 = (s32[36]{0:T(128)S(1)}, s32[36]{0:T(128)}, u32[]{:S(2)}) copy-start(s32[36]{0:T(128)} %constant.238) | copy-start | bytes 436
  7.2 3.4 copy-start.4
  7.2 19.1 %copy-start.7 = (s32[4]{0:T(128)S(1)}, s32[4]{0:T(128)}, u32[]{:S(2)}) copy-start(s32[4]{0:T(128)} %param.12) | copy-start | bytes 52
  7.2 56.9 %all-gather.3.cloned.1.call-start = ((), (), s32[]{:S(2)}) async-start(), calls=%async_computation.3 | async-start | bytes 5242880 | tf_op jit(solution)/shard_map/all_gather | solution.py:30
  9.8 585.3 %all-gather.5.cloned.1.call-start = ((), (), s32[]{:S(2)}) async-start(), calls=%async_computation.4 | async-start | bytes 10485760 | tf_op jit(solution)/shard_map/all_gather | solution.py:38
  13.6 668.5 %all-to-all-start = ((s32[64,3,1]{1,2,0:T(1,128)}), s32[64,3,1]{1,2,0:T(1,128)S(1)}, u32[]{:S(2)}, u32[]{:S(2)}) async-start(s32[64,3,1]{1,2,0:T(1,128)} %bitcast.20), calls=%async_computation | async-start | bytes 65536 | tf_op jit(solution)/shard_map/all_to_all | solution.py:66
  73.9 2.0 copy-start.1
  580.1 4.1 copy-start.2
  610.3 6.8 copy-start
  682.1 285.3 %all-to-all-start.1 = ((f32[192,128,128]{2,1,0:T(8,128)}), f32[192,128,128]{2,1,0:T(8,128)}, u32[]{:S(2)}, u32[]{:S(2)}) async-start(f32[192,128,128]{2,1,0:T(8,128)} %scatter_fusion), calls=%async_computation.1 | async-start | bytes 25165824 | tf_op jit(solution)/shard_map/all_to_all | solution.py:65
  692.8 311.9 %reduce-scatter.2.cloned.1.call-start = ((), (), s32[]{:S(2)}) async-start(), calls=%async_computation.5 | async-start | bytes 655360 | tf_op jit(solution)/shard_map/reduce_scatter | solution.py:72
  694.2 310.5 %copy-start.3 = (f32[2,128,128]{2,1,0:T(8,128)S(1)}, f32[2,128,128]{2,1,0:T(8,128)}, u32[]{:S(2)}) copy-start(f32[2,128,128]{2,1,0:T(8,128)} %param.15) | copy-start | bytes 393220
Sparse Core Ops, SparseCore 0:
  10.4 53.6 all-gather.2
  65.9 90.4 all-gather.4
  983.9 20.7 reduce-scatter.1
where the time goes:
time: 1020 us; the launch traced here: 1010 us
  other arithmetic  482 us (47%)
  waiting for transfers between devices  329 us (32%)
  matrix products  82.2 us (8%)
  local copies, waits for them, and re-layouts  82 us (8%)
  starting transfers between devices  23.3 us (2%)
  between operations  14.6 us (1%)
    another operation x16, other arithmetic, local(): factor = jnp.linalg.cholesky(whole_diag)  309 us
    all_to_all x1, waiting for transfers between devices, local(): lax.all_to_all(send_buffer, 'wide', split_axis=0, concat_axis=0, tiled=True)  273 us
    another operation x3, other arithmetic, local(): lax.linalg.triangular_solve(factor, identity, left_side=True, lower=True)  165 us
    all_gather x1, waiting for transfers between devices, local(): whole_diag = lax.all_gather(diag_block, 'narrow', axis=2, tiled=True)  36.9 us
    scatter x1, local copies, waits for them, and re-layouts, local(): jnp.zeros((buffer_rows, B, B), jnp.float32).at[position]  26.3 us
    dot_general x1, matrix products, local(): jnp.einsum('spac,spbc->spab', blocks[:, first], blocks[:, second], precis...  25.8 us
  transfers between devices with their start and end apart: 5, of which 3 were waited for; matrix products, arithmetic and copies ran while one was open for 61% of the time, Pallas kernels for 0%

commit v1 on v0

--- a/solution.py
+++ b/solution.py
@@ -27,7 +27,26 @@
     narrow_count = lax.axis_size("narrow")
     wide_count = lax.axis_size("wide")
     col_start = narrow_index * col_width
-    whole_diag = lax.all_gather(diag_block, "narrow", axis=2, tiled=True)
+    count_2, here, rows = (lax.axis_size("narrow"), lax.axis_index("narrow"), diag_block.shape[2])
+    upward = [(i, (i + 1) % count_2) for i in range(count_2)]
+    behind = [(i, (i - 1) % count_2) for i in range(count_2)]
+    out = jnp.zeros(
+        (*diag_block.shape[:2], count_2 * rows, *diag_block.shape[2 + 1 :]), diag_block.dtype
+    )
+    out = lax.dynamic_update_slice_in_dim(out, diag_block, here * rows, axis=2)
+    from_left = from_right = diag_block
+    halfway = count_2 // 2
+    for step in range(1, halfway + 1):
+        from_left = lax.ppermute(from_left, "narrow", upward)
+        out = lax.dynamic_update_slice_in_dim(
+            out, from_left, (here - step) % count_2 * rows, axis=2
+        )
+        if step < count_2 - halfway:
+            from_right = lax.ppermute(from_right, "narrow", behind)
+            out = lax.dynamic_update_slice_in_dim(
+                out, from_right, (here + step) % count_2 * rows, axis=2
+            )
+    whole_diag = out
     factor = jnp.linalg.cholesky(whole_diag)
     identity = jnp.broadcast_to(jnp.eye(W, dtype=jnp.float32), factor.shape)
     inverse = lax.linalg.triangular_solve(factor, identity, left_side=True, lower=True)

time: 1020 us -> 1050 us (1.029)
  waiting for transfers between devices: 329 us -> 349 us
  local copies, waits for them, and re-layouts: 82 us -> 92.7 us
    ppermute x0 -> x3, waiting for transfers between devices: none -> 58.3 us  [the longest x2 58.3 us: local(): from_left = lax.ppermute(from_left, 'narrow', upward)]
    all_gather x1 -> x0, waiting for transfers between devices: 36.9 us -> none  [local(): whole_diag = lax.all_gather(diag_block, 'narrow', axis=2, tiled=True)]
    dynamic_update_slice x0 -> x5, local copies, waits for them, and re-layouts: none -> 10.7 us  [the longest x3 8.61 us: local(): lax.dynamic_update_slice_in_dim(out, from_left, (here - step) % count_2 *...]
  transfers between devices with their start and end apart: 5 -> 7, of which waited for: 3 -> 4; matrix products, arithmetic and copies ran while one was open for 61% -> 60% of each run, Pallas kernels for 0% -> 0%
where the time goes in v1:
time: 1050 us
  other arithmetic  480 us (46%)
  waiting for transfers between devices  349 us (33%)
  local copies, waits for them, and re-layouts  92.7 us (9%)
  matrix products  81.4 us (8%)
  starting transfers between devices  29 us (3%)
  between operations  15.1 us (1%)
    another operation x16, other arithmetic, local(): factor = jnp.linalg.cholesky(whole_diag)  307 us
    all_to_all x1, waiting for transfers between devices, local(): lax.all_to_all(send_buffer, 'wide', split_axis=0, concat_axis=0, tiled=True)  273 us
    another operation x3, other arithmetic, local(): lax.linalg.triangular_solve(factor, identity, left_side=True, lower=True)  165 us
    ppermute x2, waiting for transfers between devices, local(): from_left = lax.ppermute(from_left, 'narrow', upward)  58.3 us
    scatter x1, local copies, waits for them, and re-layouts, local(): jnp.zeros((buffer_rows, B, B), jnp.float32).at[position]  26.3 us
    dot_general x1, matrix products, local(): jnp.einsum('spac,spbc->spab', blocks[:, first], blocks[:, second], precis...  25.8 us
  transfers between devices with their start and end apart: 7, of which 4 were waited for; matrix products, arithmetic and copies ran while one was open for 60% of the time, Pallas kernels for 0%

profile of v1, /device:TPU:8, one launch (start us, length us, event | category | flops | bytes accessed | tf_op | source)
XLA Modules:
  0.0 1046.8 jit_solution(130999223497582267)
XLA Ops:
  15.3 12.1 %all-to-all-start = ((s32[64,3,1]{1,2,0:T(1,128)}), s32[64,3,1]{1,2,0:T(1,128)S(1)}, u32[]{:S(2)}, u32[]{:S(2)}) async-start(s32[64,3,1]{1,2,0:T(1,128)} %bitcast.20), calls=%async_computation | async-start | bytes 65536 | tf_op jit(solution)/shard_map/all_to_all | solution.py:85
  27.6 19.5 %collective-permute-done = f32[4,512,128]{1,2,0:T(8,128)S(1)} collective-permute-done((f32[4,512,128]{1,2,0:T(8,128)S(1)}, f32[4,512,128]{1,2,0:T(8,128)S(1)}, u32[]{:S(2)}, u32[]{:S(2)}) %collective-permute-start) | collective-permute-done | bytes 1048608 | tf_op jit(solution)/shard_map/ppermute | solution.py:40
  54.3 38.8 %collective-permute-done.2 = f32[4,512,128]{1,2,0:T(8,128)} collective-permute-done((f32[4,512,128]{1,2,0:T(8,128)S(1)}, f32[4,512,128]{1,2,0:T(8,128)}, u32[]{:S(2)}, u32[]{:S(2)}) %collective-permute-start.2) | collective-permute-done | bytes 1048608 | tf_op jit(solution)/shard_map/ppermute | solution.py:40
  95.3 5.3 copy.125
  107.1 46.9 %custom-call.34 = f32[4,128,128]{2,1,0:T(8,128)S(1)} custom-call(f32[4,128,128]{2,1,0:T(8,128)S(1)} %cholesky.271), custom_call_target="Cholesky" | custom-call | tf_op jit(solution)/shard_map/jit(cholesky)/cholesky | solution.py:50
  154.2 39.3 %custom-call.35 = f32[4,1,128,128]{2,3,1,0:T(8,128)S(1)} custom-call(f32[4,1,128,128]{3,2,1,0:T(8,128)S(1)} %select_bitcast_fusion.2), custom_call_target="InvertDiagBlocksLowerTriangular" | custom-call | tf_op jit(solution)/shard_map/jit(cholesky)/cholesky | solution.py:50
  197.8 47.1 %custom-call.36 = f32[4,128,128]{2,1,0:T(8,128)S(1)} custom-call(f32[4,128,128]{2,1,0:T(8,128)S(1)} %cholesky.275), custom_call_target="Cholesky" | custom-call | tf_op jit(solution)/shard_map/jit(cholesky)/cholesky | solution.py:50
  245.1 39.3 %custom-call.37 = f32[4,1,128,128]{2,3,1,0:T(8,128)S(1)} custom-call(f32[4,1,128,128]{3,2,1,0:T(8,128)S(1)} %select_bitcast_fusion.1), custom_call_target="InvertDiagBlocksLowerTriangular" | custom-call | tf_op jit(solution)/shard_map/jit(cholesky)/cholesky | solution.py:50
  290.6 47.4 %custom-call.38 = f32[4,128,128]{2,1,0:T(8,128)S(1)} custom-call(f32[4,128,128]{2,1,0:T(8,128)S(1)} %cholesky.280), custom_call_target="Cholesky" | custom-call | tf_op jit(solution)/shard_map/jit(cholesky)/cholesky | solution.py:50
  338.2 39.3 %custom-call.39 = f32[4,1,128,128]{2,3,1,0:T(8,128)S(1)} custom-call(f32[4,1,128,128]{3,2,1,0:T(8,128)S(1)} %select_bitcast_fusion), custom_call_target="InvertDiagBlocksLowerTriangular" | custom-call | tf_op jit(solution)/shard_map/jit(cholesky)/cholesky | solution.py:50
  382.4 46.9 %custom-call.40 = f32[4,128,128]{2,1,0:T(8,128)S(1)} custom-call(f32[4,128,128]{2,1,0:T(8,128)S(1)} %slice_subtract_fusion.2), custom_call_target="Cholesky" | custom-call | tf_op jit(solution)/shard_map/jit(cholesky)/cholesky | solution.py:50
  430.6 6.7 broadcast_select_fusion
  437.4 15.9 %while.1 = (s32[]{:T(128)}, f32[4,512,512]{1,2,0:T(8,128)}, s32[4,2]{0,1:T(2,128)S(1)}, f32[4,4,128,128]{3,2,0,1:T(8,128)}, s32[]{:T(128)}) while((s32[]{:T(128)}, f32[4,512,512]{1,2,0:T(8,128)}, s32[4,2]{0,1:T(2,128)S(1)}, f32[4,4,128,128]{3,2,0,1:T(8,128)}, s32[]{:T(128)}) %tuple.40), condition=%wide.while_cond, body=%wide.while_body.sunk | while | flops 2 | bytes 1572981 | solution.py:52
  453.3 158.2 %custom-call.41 = f32[4,4,128,128]{2,3,1,0:T(8,128)S(1)} custom-call(f32[4,4,128,128]{3,2,1,0:T(8,128)} %bitcast.98), custom_call_target="InvertDiagBlocksLowerTriangular" | custom-call | tf_op jit(solution)/shard_map/triangular_solve | solution.py:52
  626.8 13.3 %multiply_bitcast_fusion = f32[4,1024,128]{1,2,0:T(8,128)} fusion(f32[4,1024,512]{2,1,0:T(8,128)} %all-gather.2.cloned.1.call-done, s32[]{:T(128)S(6)} %select_n.53, f32[4,128,512]{2,1,0:T(8,128)S(1)} %fusion.37, f32[4,128,512]{2,1,0:T(8,128)S(1)} %fusion.42, f32[4,128,512]{2,1,0:T(8,128)S(1)} %fusion.40, f32[4,128,512]{2,1,0:T(8,128)} %fusion.39, ...), kind=kOutput, calls=%fused_computation.29 | convolution fusion | flops 3222536192 | bytes 14696452 | tf_op jit(solution)/shard_map/srk,skc->src/dot_general | solution.py:55
  642.0 6.7 gather_fusion.1
  648.7 6.7 gather_fusion
  655.4 25.8 %fusion.2 = f32[4,36,128,128]{3,2,1,0:T(8,128)} fusion(f32[36,4,128,128]{3,2,1,0:T(8,128)} %gather_fusion.1, f32[36,4,128,128]{3,2,1,0:T(8,128)} %gather_fusion), kind=kOutput, calls=%fused_computation.9 | convolution fusion | flops 3623878656 | bytes 28311552 | tf_op jit(solution)/shard_map/spac,spbc->spab/dot_general | solution.py:66
  681.2 6.2 broadcast_in_dim.47
  687.4 26.3 %scatter_fusion = f32[192,128,128]{2,1,0:T(8,128)} fusion(f32[192,128,128]{2,1,0:T(8,128)} %broadcast_in_dim.47, s32[144]{0:T(256)S(1)} %bitcast.96, f32[144,128,128]{2,1,0:T(8,128)} %bitcast.92), kind=kCustom, calls=%fused_computation.3 | custom fusion | bytes 28312128 | tf_op jit(solution)/shard_map/scatter | solution.py:82
  713.7 13.8 %all-to-all-start.1 = ((f32[192,128,128]{2,1,0:T(8,128)}), f32[192,128,128]{2,1,0:T(8,128)}, u32[]{:S(2)}, u32[]{:S(2)}) async-start(f32[192,128,128]{2,1,0:T(8,128)} %scatter_fusion), calls=%async_computation.1 | async-start | bytes 25165824 | tf_op jit(solution)/shard_map/all_to_all | solution.py:84
  728.9 273.1 %all-to-all-done.1 = f32[192,128,128]{2,1,0:T(8,128)} async-done(((f32[192,128,128]{2,1,0:T(8,128)}), f32[192,128,128]{2,1,0:T(8,128)}, u32[]{:S(2)}, u32[]{:S(2)}) %all-to-all-start.1) | async-done | bytes 12582944 | tf_op jit(solution)/shard_map/all_to_all | solution.py:84
  1002.0 15.5 %fusion = f32[8,128,128]{2,0,1:T(8,128)S(1)} fusion(f32[192,128,128]{2,1,0:T(8,128)} %all-to-all-done.1, s32[192]{0:T(256)S(1)} %eq.58), kind=kOutput, calls=%fused_computation.7 | convolution fusion | flops 301991424 | bytes 13107968 | tf_op jit(solution)/shard_map/ri,rab->iab/dot_general | solution.py:90
  1021.1 16.9 %reduce-scatter.2.cloned.1.call-done = f32[2,128,128]{2,1,0:T(8,128)} async-done(((f32[8,128,128]{2,1,0:T(8,128)}), f32[2,128,128]{2,1,0:T(8,128)}) %reduce-scatter.2.cloned.1.call-update) | async-done | bytes 131088 | tf_op jit(solution)/shard_map/reduce_scatter | solution.py:91
  (127 shorter events, 80.5 us)
Async XLA Ops:
  7.2 20.3 %copy-start.11 = (s32[36]{0:T(128)S(1)}, s32[36]{0:T(128)}, u32[]{:S(2)}) copy-start(s32[36]{0:T(128)} %constant.262) | copy-start | bytes 436
  7.2 20.4 %copy-start.10 = (s32[36]{0:T(128)S(1)}, s32[36]{0:T(128)}, u32[]{:S(2)}) copy-start(s32[36]{0:T(128)} %constant.263) | copy-start | bytes 436
  7.2 5.2 copy-start.9
  7.2 619.6 %all-gather.2.cloned.1.call-start = ((), (), s32[]{:S(2)}) async-start(), calls=%async_computation.3 | async-start | bytes 10485760 | tf_op jit(solution)/shard_map/all_gather | solution.py:57
  9.5 41.6 %copy-start.12 = (s32[4]{0:T(128)S(1)}, s32[4]{0:T(128)}, u32[]{:S(2)}) copy-start(s32[4]{0:T(128)} %param.12) | copy-start | bytes 52
  9.5 43.7 %collective-permute-start.1 = (f32[4,512,128]{1,2,0:T(8,128)S(1)}, f32[4,512,128]{1,2,0:T(8,128)S(1)}, u32[]{:S(2)}, u32[]{:S(2)}) collective-permute-start(f32[4,512,128]{1,2,0:T(8,128)S(1)} %copy.122), channel_id=1, source_target_pairs={{0,3},{1,0},{2,1},{3,2},{4,7},{5,4},{6,5},{7,6},{8,11},{9,8},{10,9... | collective-permute-start | bytes 3145736 | tf_op jit(solution)/shard_map/ppermute | solution.py:45
  12.3 34.8 %collective-permute-start = (f32[4,512,128]{1,2,0:T(8,128)S(1)}, f32[4,512,128]{1,2,0:T(8,128)S(1)}, u32[]{:S(2)}, u32[]{:S(2)}) collective-permute-start(f32[4,512,128]{1,2,0:T(8,128)S(1)} %copy.122), channel_id=1, source_target_pairs={{0,1},{1,2},{2,3},{3,0},{4,5},{5,6},{6,7},{7,4},{8,9},{9,10},{10,1... | collective-permute-start | bytes 3145736 | tf_op jit(solution)/shard_map/ppermute | solution.py:40
  15.3 698.3 %all-to-all-start = ((s32[64,3,1]{1,2,0:T(1,128)}), s32[64,3,1]{1,2,0:T(1,128)S(1)}, u32[]{:S(2)}, u32[]{:S(2)}) async-start(s32[64,3,1]{1,2,0:T(1,128)} %bitcast.20), calls=%async_computation | async-start | bytes 65536 | tf_op jit(solution)/shard_map/all_to_all | solution.py:85
  47.2 45.9 %collective-permute-start.2 = (f32[4,512,128]{1,2,0:T(8,128)S(1)}, f32[4,512,128]{1,2,0:T(8,128)}, u32[]{:S(2)}, u32[]{:S(2)}) collective-permute-start(f32[4,512,128]{1,2,0:T(8,128)S(1)} %collective-permute-done), channel_id=1, source_target_pairs={{0,1},{1,2},{2,3},{3,0},{4,5},{5,6},{6,7},{7,4},{8,9},{9,10},{10,1... | collective-permute-start | bytes 3145736 | tf_op jit(solution)/shard_map/ppermute | solution.py:40
  105.1 2.0 copy-start.2
  285.7 2.0 copy-start.1
  437.4 174.2 %copy-start.6 = (f32[128,512]{1,0:T(8,128)S(1)}, f32[128,512]{1,0:T(8,128)}, u32[]{:S(2)}) copy-start(f32[128,512]{1,0:T(8,128)} %get-tuple-element.58) | copy-start | bytes 786436
  437.4 175.2 %copy-start.5 = (f32[128,512]{1,0:T(8,128)S(1)}, f32[128,512]{1,0:T(8,128)}, u32[]{:S(2)}) copy-start(f32[128,512]{1,0:T(8,128)} %get-tuple-element.57) | copy-start | bytes 786436
  453.3 162.5 %copy-start.7 = (f32[128,512]{1,0:T(8,128)S(1)}, f32[128,512]{1,0:T(8,128)}, u32[]{:S(2)}) copy-start(f32[128,512]{1,0:T(8,128)} %get-tuple-element.56) | copy-start | bytes 786436
  611.5 4.2 copy-start.3
  614.7 5.6 copy-start.4
  641.9 6.8 copy-start
  713.7 288.4 %all-to-all-start.1 = ((f32[192,128,128]{2,1,0:T(8,128)}), f32[192,128,128]{2,1,0:T(8,128)}, u32[]{:S(2)}, u32[]{:S(2)}) async-start(f32[192,128,128]{2,1,0:T(8,128)} %scatter_fusion), calls=%async_computation.1 | async-start | bytes 25165824 | tf_op jit(solution)/shard_map/all_to_all | solution.py:84
  727.5 310.4 %reduce-scatter.2.cloned.1.call-start = ((), (), s32[]{:S(2)}) async-start(), calls=%async_computation.4 | async-start | bytes 655360 | tf_op jit(solution)/shard_map/reduce_scatter | solution.py:91
  1017.5 20.4 %copy-start.8 = (f32[2,128,128]{2,1,0:T(8,128)S(1)}, f32[2,128,128]{2,1,0:T(8,128)}, u32[]{:S(2)}) copy-start(f32[2,128,128]{2,1,0:T(8,128)} %param.15) | copy-start | bytes 393220
Sparse Core Ops, SparseCore 0:
  9.8 119.3 all-gather.1
  1018.6 19.3 reduce-scatter.1
